TPU v7x, 512 devices: a whole 4x8x8 slice. The times are simulated.
512 devices in a mesh: dom: 32 (over z, x), band: 16 (over y, core).
Axes of the slice: x: 4, y: 8, z: 8, core: 2. Of those that a mesh axis runs over, the one named last changes fastest.
Arguments:
- waves: float32 [256, 131072], P('band', 'dom'), may hold values from -6 to 6
- potential: float32 [131072], P('dom'), may hold values from 0 to 4
- atom_points: int32 [128, 256], P('dom'), may hold values from 0 to 4095
- projectors: float32 [128, 8, 256], P('dom'), may hold values from -0.75 to 0.75
- coupling: float32 [128, 8, 8], P('dom'), may hold values from -1 to 1
Outputs:
- ortho: float32 [256, 131072], P('band', 'dom')
Inputs may be any that keep to these rules, and one draw needn't show every extreme that they name: `atom_points`: an index of a point within the atom's own subdomain, repeats allowed.
All inputs are finite; a program needn't handle non-finite values.
Results may differ from a plain program's by a relative error of at most 0.0003.
Values sent between devices are 32-bit elements; how exact they have to be, the bound alone decides.
A program may use at most 64 MiB of HBM per device.

v0:
```python
import jax
import jax.numpy as jnp
from jax import lax
from jax.sharding import PartitionSpec as P

CUBE = 16
high = lax.Precision.HIGHEST


def passed_along(value, axis, by):
    size = lax.axis_size(axis)
    pairs = [(i, i + by) for i in range(size) if 0 <= i + by < size]
    return lax.ppermute(value, axis, pairs)


def shifted(face, offset):
    return passed_along(face, "dom", offset)


def laplace(grid, coords, counts, strides):
    total = -7.5 * grid
    for dim in range(3):
        axis = dim + 1
        lower_face = lax.slice_in_dim(grid, 0, 2, axis=axis)
        upper_face = lax.slice_in_dim(grid, CUBE - 2, CUBE, axis=axis)
        above = shifted(lower_face, -strides[dim]) * (coords[dim] < counts[dim] - 1).astype(
            jnp.float32
        )
        below = shifted(upper_face, strides[dim]) * (coords[dim] > 0).astype(jnp.float32)
        padded = jnp.concatenate([below, grid, above], axis=axis)

        def part(offset):
            return lax.slice_in_dim(padded, offset, offset + CUBE, axis=axis)

        total = total + 4.0 / 3.0 * (part(1) + part(3)) - 1.0 / 12.0 * (part(0) + part(4))
    return total


def nonlocal_one(values, points, proj, coup):
    picked = values[:, points]
    coef = jnp.einsum("aks,bas->bak", proj, picked, precision=high)
    mixed = jnp.einsum("akj,baj->bak", coup, coef, precision=high)
    spread = jnp.einsum("aks,bak->bas", proj, mixed, precision=high)
    return jnp.zeros_like(values).at[:, points.reshape(-1)].add(spread.reshape(values.shape[0], -1))


def local(waves, potential, atom_points, projectors, coupling):
    groups, local_points = waves.shape
    dom_count = lax.axis_size("dom")
    depth_z = 2
    depth_y = min(4, dom_count // 2)
    depth_x = dom_count // (depth_z * depth_y)
    where = lax.axis_index("dom")
    coords = (where // (depth_y * depth_z), where // depth_z % depth_y, where % depth_z)
    counts = (depth_x, depth_y, depth_z)
    strides = (depth_y * depth_z, depth_z, 1)

    def apply_h(values):
        grid = values.reshape(groups, CUBE, CUBE, CUBE)
        kinetic = laplace(grid, coords, counts, strides).reshape(groups, local_points)
        extra = nonlocal_one(values, atom_points, projectors, coupling)
        return -0.5 * kinetic + potential[None, :] * values + extra

    first = (apply_h(waves) - 6.0 * waves) / 4.0
    filtered = 2.0 * (apply_h(first) - 6.0 * first) / 4.0 - waves
    pieces = lax.all_to_all(filtered, "band", split_axis=1, concat_axis=0, tiled=True)
    scale = 1.0 / (dom_count * local_points)
    partial_value = (
        jnp.dot(pieces, pieces.T, precision=high, preferred_element_type=jnp.float32) * scale
    )
    gram = lax.psum(partial_value, ("dom", "band"))
    lower = jnp.linalg.cholesky(gram)
    rotated = jax.scipy.linalg.solve_triangular(lower, pieces, lower=True)
    return lax.all_to_all(rotated, "band", split_axis=0, concat_axis=1, tiled=True)


def solution(mesh):
    placed = (
        P("band", "dom"),
        P("dom"),
        P("dom", None),
        P("dom", None, None),
        P("dom", None, None),
    )
    return jax.shard_map(
        local, mesh=mesh, in_specs=placed, out_specs=P("band", "dom"), check_vma=False
    )
```

profile of v0, /device:TPU:1, one launch (start us, length us, event | category | flops | bytes accessed | tf_op | source)
XLA Modules:
  0.0 548.6 jit_solution(12536738940076583858)
XLA Ops:
  6.5 1.7 reshape.78
  8.2 2.7 fusion.58
  10.9 3.1 copy.102
  14.0 4.6 collective-permute-start.4
  18.7 3.9 copy.105
  22.6 1.4 collective-permute-start.5
  24.0 1.1 fusion.59
  25.1 5.5 %collective-permute-start.2 = (f32[16,16,2,16]{3,2,1,0:T(2,128)}, f32[16,16,2,16]{3,2,1,0:T(2,128)}, u32[]{:S(2)}, u32[]{:S(2)}) collective-permute-start(f32[16,16,2,16]{3,2,1,0:T(2,128)} %get-tuple-element.31), channel_id=1, source_target_pairs={{0,32},{16,48},{32,64},{48,80},{64,96},{80,112},{96,128},{112,144}... | collective-permute-start | bytes 98312 | tf_op jit(solution)/shard_map/ppermute | solution.py:13
  30.6 1.4 collective-permute-start.3
  32.9 9.7 %collective-permute-start = (f32[16,2,16,16]{3,2,1,0:T(8,128)}, f32[16,2,16,16]{3,2,1,0:T(8,128)}, u32[]{:S(2)}, u32[]{:S(2)}) collective-permute-start(f32[16,2,16,16]{3,2,1,0:T(8,128)} %get-tuple-element.33), channel_id=1, source_target_pairs={{0,128},{16,144},{32,160},{48,176},{64,192},{80,208},{96,224},{112... | collective-permute-start | bytes 98312 | tf_op jit(solution)/shard_map/ppermute | solution.py:13
  42.6 2.0 copy.108
  44.6 4.4 gather_fusion
  50.5 1.0 copy.112
  51.5 1.3 collective-permute-start.1
  52.8 1.0 broadcast_multiply_fusion.8
  53.8 1.0 broadcast_multiply_fusion.3
  54.8 1.7 broadcast_multiply_fusion.1
  56.5 1.0 broadcast_multiply_fusion.12
  57.4 2.9 copy.104
  60.3 3.8 copy.107
  64.2 7.2 %collective-permute-done.1 = f32[16,2,16,16]{3,2,1,0:T(8,128)} collective-permute-done((f32[16,2,16,16]{3,2,1,0:T(8,128)}, f32[16,2,16,16]{3,2,1,0:T(8,128)}, u32[]{:S(2)}, u32[]{:S(2)}) %collective-permute-start.1) | collective-permute-done | bytes 32800 | tf_op jit(solution)/shard_map/ppermute | solution.py:13
  71.4 1.0 broadcast_multiply_fusion.10
  72.3 8.1 %fusion.20 = f32[16,16,16,16]{3,2,1,0:T(8,128)} fusion(f32[16,16,16,16]{3,2,1,0:T(8,128)S(1)} %reshape.78, f32[16,2,16,16]{3,2,1,0:T(8,128)S(1)} %broadcast_multiply_fusion.10, f32[16,2,16,16]{3,2,1,0:T(8,128)S(1)} %broadcast_multiply_fusion.12, f32[16,16,2,16]{3,2,1,0:T(2,128)S(1)} %bitcast.110, f32[16,16,2,16]{3,2,1,0:T(2,128)S(1)} %bitcast.108, ...), kind=kLoop, calls=%fused_computation.42 | loop fusion | flops 2097152 | bytes 720896 | tf_op jit(solution)/shard_map/mul | solution.py:62
  80.4 3.1 mul.170
  84.3 7.6 %scatter_fusion = f32[16,4096]{0,1:T(8,128)S(1)} fusion(f32[16,4096]{0,1:T(8,128)S(1)} %copy.111, s32[1024]{0:T(1024)S(1)} %bitcast.121, f32[1024,16]{1,0:T(8,128)} %copy.112), kind=kCustom, calls=%fused_computation.2 | custom fusion | flops 16384 | bytes 200704 | tf_op jit(solution)/shard_map/scatter-add | solution.py:44
  93.3 2.8 fusion.55
  96.0 1.0 fusion.56
  97.1 0.8 fusion.57
  97.9 2.0 copy.120
  99.9 3.1 copy.114
  103.0 2.0 collective-permute-start.10
  105.0 3.9 copy.117
  108.9 1.3 collective-permute-start.11
  110.2 4.0 collective-permute-start.8
  114.2 1.3 collective-permute-start.9
  115.5 13.4 %collective-permute-start.6 = (f32[16,2,16,16]{3,2,1,0:T(8,128)}, f32[16,2,16,16]{3,2,1,0:T(8,128)}, u32[]{:S(2)}, u32[]{:S(2)}) collective-permute-start(f32[16,2,16,16]{3,2,1,0:T(8,128)} %get-tuple-element.27), channel_id=1, source_target_pairs={{0,128},{16,144},{32,160},{48,176},{64,192},{80,208},{96,224},{112... | collective-permute-start | bytes 98312 | tf_op jit(solution)/shard_map/ppermute | solution.py:13
  128.9 4.4 gather_fusion.1
  134.1 1.0 copy.124
  135.1 1.3 collective-permute-start.7
  136.4 1.0 broadcast_multiply_fusion.7
  137.4 1.0 broadcast_multiply_fusion.5
  138.4 1.0 broadcast_multiply_fusion.2
  139.3 1.7 broadcast_multiply_fusion
  141.0 1.7 broadcast_multiply_fusion.11
  142.7 2.9 copy.116
  145.6 3.9 copy.119
  149.5 1.0 broadcast_multiply_fusion.9
  150.5 8.1 %fusion.9 = f32[16,16,16,16]{3,2,1,0:T(8,128)} fusion(f32[16,16,16,16]{3,2,1,0:T(8,128)S(1)} %reshape.81, f32[16,2,16,16]{3,2,1,0:T(8,128)S(1)} %broadcast_multiply_fusion.9, f32[16,2,16,16]{3,2,1,0:T(8,128)S(1)} %copy-done.2, f32[16,16,2,16]{3,2,1,0:T(2,128)S(1)} %bitcast.109, f32[16,16,2,16]{3,2,1,0:T(2,128)S(1)} %bitcast.107, ...), kind=kLoop, calls=%fused_computation.31 | loop fusion | flops 2097152 | bytes 720896 | tf_op jit(solution)/shard_map/mul | solution.py:62
  158.6 3.1 mul.188
  162.4 7.2 %scatter_fusion.1 = f32[16,4096]{0,1:T(8,128)S(1)} fusion(f32[16,4096]{0,1:T(8,128)S(1)} %copy.123, s32[1024]{0:T(1024)S(1)} %bitcast.122, f32[1024,16]{1,0:T(8,128)} %copy.124), kind=kCustom, calls=%fused_computation.3 | custom fusion | flops 16384 | bytes 200704 | tf_op jit(solution)/shard_map/scatter-add | solution.py:44
  170.9 9.0 %all-to-all-start = ((f32[16,16,256]{2,0,1:T(8,128)}), f32[16,16,256]{2,0,1:T(8,128)S(1)}, u32[]{:S(2)}, u32[]{:S(2)}) async-start(f32[16,16,256]{2,0,1:T(8,128)} %bitcast.90), calls=%async_computation | async-start | bytes 524288 | tf_op jit(solution)/shard_map/all_to_all | solution.py:66
  180.2 11.3 %all-to-all-done = f32[16,16,256]{2,0,1:T(8,128)S(1)} async-done(((f32[16,16,256]{2,0,1:T(8,128)}), f32[16,16,256]{2,0,1:T(8,128)S(1)}, u32[]{:S(2)}, u32[]{:S(2)}) %all-to-all-start) | async-done | bytes 262176 | tf_op jit(solution)/shard_map/all_to_all | solution.py:66
  191.5 1.1 convolution_multiply_fusion
  192.7 267.4 %all-reduce.3.cloned.1.call-done = f32[256,256]{0,1:T(8,128)} async-done(((f32[256,256]{0,1:T(8,128)}), f32[256,256]{0,1:T(8,128)}) %all-reduce.3.cloned.1.call-update) | async-done | bytes 262160 | tf_op jit(solution)/shard_map/psum | solution.py:71
  460.1 1.1 copy.128
  461.2 1.0 fusion.44
  462.2 11.7 %cholesky.50 = f32[128,128]{1,0:T(8,128)S(1)} custom-call(f32[128,128]{1,0:T(8,128)S(1)} %cholesky.118), custom_call_target="Cholesky" | custom-call | tf_op jit(solution)/shard_map/jit(cholesky)/cholesky | solution.py:72
  474.0 9.8 %custom-call.15 = f32[1,128,128]{1,2,0:T(8,128)S(1)} custom-call(f32[1,128,128]{2,1,0:T(8,128)S(1)} %get-tuple-element.40), custom_call_target="InvertDiagBlocksLowerTriangular" | custom-call | tf_op jit(solution)/shard_map/jit(cholesky)/cholesky | solution.py:72
  484.3 11.7 %cholesky.105 = f32[128,128]{1,0:T(8,128)S(1)} custom-call(f32[128,128]{1,0:T(8,128)S(1)} %convolution_subtract_fusion.1), custom_call_target="Cholesky" | custom-call | tf_op jit(solution)/shard_map/jit(cholesky)/cholesky | solution.py:72
  498.2 4.3 while.1
  499.0 1.4 bitcast_dynamic-update-slice_fusion.2
  501.0 1.4 bitcast_dynamic-update-slice_fusion.2
  502.5 19.7 %custom-call.16 = f32[2,128,128]{1,2,0:T(8,128)S(1)} custom-call(f32[2,128,128]{2,1,0:T(8,128)S(1)} %get-tuple-element.12), custom_call_target="InvertDiagBlocksLowerTriangular" | custom-call | tf_op jit(solution)/shard_map/jit(_solve_triangular)/triangular_solve | solution.py:73
  523.1 17.7 %all_to_all.38 = f32[16,16,256]{2,1,0:T(8,128)S(1)} all-to-all(f32[16,16,256]{2,1,0:T(8,128)S(1)} %bitcast.111), channel_id=1, replica_groups=mesh['dom'=32,'band'=16] {'band'}, dimensions={0} | all-to-all | bytes 524288 | tf_op jit(solution)/shard_map/all_to_all | solution.py:74
  (82 shorter events, 11.6 us)
Async XLA Ops:
  6.5 43.2 %copy-start = (f32[4,8,256]{2,1,0:T(8,128)S(1)}, f32[4,8,256]{2,1,0:T(8,128)}, u32[]{:S(2)}) copy-start(f32[4,8,256]{2,1,0:T(8,128)} %param.8) | copy-start | bytes 98308
  14.0 39.8 %collective-permute-start.4 = (f32[16,16,16,2]{2,1,3,0:T(8,128)S(1)}, f32[16,16,16,2]{2,1,3,0:T(8,128)}, u32[]{:S(2)}, u32[]{:S(2)}) collective-permute-start(f32[16,16,16,2]{2,1,3,0:T(8,128)S(1)} %copy.102), channel_id=1, source_target_pairs={{0,16},{16,32},{32,48},{48,64},{64,80},{80,96},{96,112},{112,128},... | collective-permute-start | bytes 98312 | tf_op jit(solution)/shard_map/ppermute | solution.py:13
  18.7 23.9 %copy-start.1 = (f32[16,4096]{1,0:T(8,128)S(1)}, f32[16,4096]{1,0:T(8,128)}, u32[]{:S(2)}) copy-start(f32[16,4096]{1,0:T(8,128)} %param.5) | copy-start | bytes 786436
  22.6 22.0 %copy-start.9 = (s32[4,256]{1,0:T(4,128)S(1)}, s32[4,256]{1,0:T(4,128)}, u32[]{:S(2)}) copy-start(s32[4,256]{1,0:T(4,128)} %param.7) | copy-start | bytes 12292
  22.6 32.2 %collective-permute-start.5 = (f32[16,16,16,2]{2,1,3,0:T(8,128)}, f32[16,16,16,2]{2,1,3,0:T(8,128)}, u32[]{:S(2)}, u32[]{:S(2)}) collective-permute-start(f32[16,16,16,2]{2,1,3,0:T(8,128)} %copy.105), channel_id=1, source_target_pairs={{16,0},{32,16},{48,32},{64,48},{80,64},{96,80},{112,96},{128,112},... | collective-permute-start | bytes 98312 | tf_op jit(solution)/shard_map/ppermute | solution.py:13
  25.1 26.4 %collective-permute-start.2 = (f32[16,16,2,16]{3,2,1,0:T(2,128)}, f32[16,16,2,16]{3,2,1,0:T(2,128)}, u32[]{:S(2)}, u32[]{:S(2)}) collective-permute-start(f32[16,16,2,16]{3,2,1,0:T(2,128)} %get-tuple-element.31), channel_id=1, source_target_pairs={{0,32},{16,48},{32,64},{48,80},{64,96},{80,112},{96,128},{112,144}... | collective-permute-start | bytes 98312 | tf_op jit(solution)/shard_map/ppermute | solution.py:13
  30.6 19.1 %copy-start.4 = (f32[4096]{0:T(1024)S(1)}, f32[4096]{0:T(1024)}, u32[]{:S(2)}) copy-start(f32[4096]{0:T(1024)} %param.6) | copy-start | bytes 49156
  30.6 23.1 %collective-permute-start.3 = (f32[16,16,2,16]{3,2,1,0:T(2,128)}, f32[16,16,2,16]{3,2,1,0:T(2,128)S(1)}, u32[]{:S(2)}, u32[]{:S(2)}) collective-permute-start(f32[16,16,2,16]{3,2,1,0:T(2,128)} %get-tuple-element.32), channel_id=1, source_target_pairs={{32,0},{48,16},{64,32},{80,48},{96,64},{112,80},{128,96},{144,112}... | collective-permute-start | bytes 98312 | tf_op jit(solution)/shard_map/ppermute | solution.py:13
  32.9 17.1 %copy-start.3 = (f32[4,8,8]{2,1,0:T(8,128)S(1)}, f32[4,8,8]{2,1,0:T(8,128)}, u32[]{:S(2)}) copy-start(f32[4,8,8]{2,1,0:T(8,128)} %param.9) | copy-start | bytes 3076
  32.9 23.6 %collective-permute-start = (f32[16,2,16,16]{3,2,1,0:T(8,128)}, f32[16,2,16,16]{3,2,1,0:T(8,128)}, u32[]{:S(2)}, u32[]{:S(2)}) collective-permute-start(f32[16,2,16,16]{3,2,1,0:T(8,128)} %get-tuple-element.33), channel_id=1, source_target_pairs={{0,128},{16,144},{32,160},{48,176},{64,192},{80,208},{96,224},{112... | collective-permute-start | bytes 98312 | tf_op jit(solution)/shard_map/ppermute | solution.py:13
  44.6 4.6 copy-start.7
  51.5 19.9 %collective-permute-start.1 = (f32[16,2,16,16]{3,2,1,0:T(8,128)}, f32[16,2,16,16]{3,2,1,0:T(8,128)}, u32[]{:S(2)}, u32[]{:S(2)}) collective-permute-start(f32[16,2,16,16]{3,2,1,0:T(8,128)} %get-tuple-element.34), channel_id=1, source_target_pairs={{128,0},{144,16},{160,32},{176,48},{192,64},{208,80},{224,96},{240... | collective-permute-start | bytes 98312 | tf_op jit(solution)/shard_map/ppermute | solution.py:13
  83.6 0.7 copy-start.5
  99.9 29.0 %copy-start.8 = (s32[1024]{0:T(1024)S(1)}, s32[1024]{0:T(1024)}, u32[]{:S(2)}) copy-start(s32[1024]{0:T(1024)} %copy-done.7) | copy-start | bytes 12292
  103.0 35.3 %collective-permute-start.10 = (f32[16,16,16,2]{2,1,3,0:T(8,128)S(1)}, f32[16,16,16,2]{2,1,3,0:T(8,128)}, u32[]{:S(2)}, u32[]{:S(2)}) collective-permute-start(f32[16,16,16,2]{2,1,3,0:T(8,128)S(1)} %copy.114), channel_id=1, source_target_pairs={{0,16},{16,32},{32,48},{48,64},{64,80},{80,96},{96,112},{112,128},... | collective-permute-start | bytes 98312 | tf_op jit(solution)/shard_map/ppermute | solution.py:13
  108.9 30.4 %collective-permute-start.11 = (f32[16,16,16,2]{2,1,3,0:T(8,128)}, f32[16,16,16,2]{2,1,3,0:T(8,128)}, u32[]{:S(2)}, u32[]{:S(2)}) collective-permute-start(f32[16,16,16,2]{2,1,3,0:T(8,128)} %copy.117), channel_id=1, source_target_pairs={{16,0},{32,16},{48,32},{64,48},{80,64},{96,80},{112,96},{128,112},... | collective-permute-start | bytes 98312 | tf_op jit(solution)/shard_map/ppermute | solution.py:13
  110.2 24.9 %collective-permute-start.8 = (f32[16,16,2,16]{3,2,1,0:T(2,128)}, f32[16,16,2,16]{3,2,1,0:T(2,128)}, u32[]{:S(2)}, u32[]{:S(2)}) collective-permute-start(f32[16,16,2,16]{3,2,1,0:T(2,128)} %get-tuple-element.25), channel_id=1, source_target_pairs={{0,32},{16,48},{32,64},{48,80},{64,96},{80,112},{96,128},{112,144}... | collective-permute-start | bytes 98312 | tf_op jit(solution)/shard_map/ppermute | solution.py:13
  114.2 23.1 %collective-permute-start.9 = (f32[16,16,2,16]{3,2,1,0:T(2,128)}, f32[16,16,2,16]{3,2,1,0:T(2,128)}, u32[]{:S(2)}, u32[]{:S(2)}) collective-permute-start(f32[16,16,2,16]{3,2,1,0:T(2,128)} %get-tuple-element.26), channel_id=1, source_target_pairs={{32,0},{48,16},{64,32},{80,48},{96,64},{112,80},{128,96},{144,112}... | collective-permute-start | bytes 98312 | tf_op jit(solution)/shard_map/ppermute | solution.py:13
  115.5 25.5 %collective-permute-start.6 = (f32[16,2,16,16]{3,2,1,0:T(8,128)}, f32[16,2,16,16]{3,2,1,0:T(8,128)}, u32[]{:S(2)}, u32[]{:S(2)}) collective-permute-start(f32[16,2,16,16]{3,2,1,0:T(8,128)} %get-tuple-element.27), channel_id=1, source_target_pairs={{0,128},{16,144},{32,160},{48,176},{64,192},{80,208},{96,224},{112... | collective-permute-start | bytes 98312 | tf_op jit(solution)/shard_map/ppermute | solution.py:13
  135.1 14.4 %collective-permute-start.7 = (f32[16,2,16,16]{3,2,1,0:T(8,128)}, f32[16,2,16,16]{3,2,1,0:T(8,128)}, u32[]{:S(2)}, u32[]{:S(2)}) collective-permute-start(f32[16,2,16,16]{3,2,1,0:T(8,128)} %get-tuple-element.28), channel_id=1, source_target_pairs={{128,0},{144,16},{160,32},{176,48},{192,64},{208,80},{224,96},{240... | collective-permute-start | bytes 98312 | tf_op jit(solution)/shard_map/ppermute | solution.py:13
  145.6 4.9 copy-start.2
  161.7 0.7 copy-start.6
  170.9 20.6 %all-to-all-start = ((f32[16,16,256]{2,0,1:T(8,128)}), f32[16,16,256]{2,0,1:T(8,128)S(1)}, u32[]{:S(2)}, u32[]{:S(2)}) async-start(f32[16,16,256]{2,0,1:T(8,128)} %bitcast.90), calls=%async_computation | async-start | bytes 524288 | tf_op jit(solution)/shard_map/all_to_all | solution.py:66
  180.0 280.2 %all-reduce.3.cloned.1.call-start = ((), (), s32[]{:S(2)}) async-start(), calls=%async_computation.2 | async-start | bytes 524288 | tf_op jit(solution)/shard_map/psum | solution.py:71
Sparse Core Ops, SparseCore 0:
  192.8 267.2 all-reduce.2
where the time goes:
time: 558 us; the launch traced here: 549 us
  waiting for transfers between devices  286 us (51%)
  other arithmetic  99.4 us (18%)
  local copies, waits for them, and re-layouts  69.6 us (12%)
  starting transfers between devices  56.5 us (10%)
  blocking collectives  17.7 us (3%)
  between operations  15.5 us (3%)
    psum x1, waiting for transfers between devices, local(): gram = lax.psum(partial_value, ('dom', 'band'))  267 us
    ppermute x12, starting transfers between devices, passed_along(): return lax.ppermute(value, axis, pairs)  47.3 us
    another operation x6, other arithmetic, local(): lower = jnp.linalg.cholesky(gram)  34 us
    another operation x4, other arithmetic, local(): rotated = jax.scipy.linalg.solve_triangular(lower, pieces, lower=True)  19.7 us
    all_to_all x1, blocking collectives, local(): lax.all_to_all(rotated, 'band', split_axis=0, concat_axis=1, tiled=True)  17.7 us
    mul x3, other arithmetic, apply_h(): return -0.5 * kinetic + potential[None, :] * values + extra  16.2 us
    slice x8, local copies, waits for them, and re-layouts, laplace(): upper_face = lax.slice_in_dim(grid, CUBE - 2, CUBE, axis=axis)  15.5 us
    scatter-add x2, other arithmetic, nonlocal_one(): jnp.zeros_like(values).at[:, points.reshape(-1)]  14.8 us
  transfers between devices with their start and end apart: 14, of which 3 were waited for; matrix products, arithmetic and copies ran while one was open for 9% of the time, Pallas kernels for 0%

commit v1 on v0

--- a/solution.py
+++ b/solution.py
@@ -68,7 +68,9 @@
     partial_value = (
         jnp.dot(pieces, pieces.T, precision=high, preferred_element_type=jnp.float32) * scale
     )
-    gram = lax.psum(partial_value, ("dom", "band"))
+    gram = partial_value
+    for h in ("band", "dom"):
+        gram = lax.psum(gram, h)
     lower = jnp.linalg.cholesky(gram)
     rotated = jax.scipy.linalg.solve_triangular(lower, pieces, lower=True)
     return lax.all_to_all(rotated, "band", split_axis=0, concat_axis=1, tiled=True)

time: 558 us -> 563 us (level)
  blocking collectives: 17.7 us -> 43.7 us
  waiting for transfers between devices: 286 us -> 275 us
  starting transfers between devices: 56.5 us -> 47.3 us
    all_to_all x0 -> x1, blocking collectives: none -> 20.5 us  [local(): lax.all_to_all(filtered, 'band', split_axis=1, concat_axis=0, tiled=True)]
    all_to_all x1 -> x0, waiting for transfers between devices: 11.3 us -> none  [local(): lax.all_to_all(filtered, 'band', split_axis=1, concat_axis=0, tiled=True)]
    all_to_all x1 -> x0, starting transfers between devices: 9.01 us -> none  [local(): lax.all_to_all(filtered, 'band', split_axis=1, concat_axis=0, tiled=True)]
    psum x1 -> x2, waiting for transfers between devices: 267 us -> 268 us  [local(): gram = lax.psum(gram, h)]
where the time goes in v1:
time: 563 us; the launch traced here: 554 us
  waiting for transfers between devices  275 us (49%)
  other arithmetic  99.4 us (18%)
  local copies, waits for them, and re-layouts  68.6 us (12%)
  starting transfers between devices  47.3 us (8%)
  blocking collectives  43.7 us (8%)
  between operations  15.4 us (3%)
    psum x2, waiting for transfers between devices, local(): gram = lax.psum(gram, h)  268 us
    ppermute x12, starting transfers between devices, passed_along(): return lax.ppermute(value, axis, pairs)  47.3 us
    another operation x6, other arithmetic, local(): lower = jnp.linalg.cholesky(gram)  33.9 us
    all_to_all x1, blocking collectives, local(): lax.all_to_all(rotated, 'band', split_axis=0, concat_axis=1, tiled=True)  23.1 us
    all_to_all x1, blocking collectives, local(): lax.all_to_all(filtered, 'band', split_axis=1, concat_axis=0, tiled=True)  20.5 us
    another operation x4, other arithmetic, local(): rotated = jax.scipy.linalg.solve_triangular(lower, pieces, lower=True)  19.7 us
    mul x3, other arithmetic, apply_h(): return -0.5 * kinetic + potential[None, :] * values + extra  16.3 us
    slice x8, local copies, waits for them, and re-layouts, laplace(): upper_face = lax.slice_in_dim(grid, CUBE - 2, CUBE, axis=axis)  15.5 us
  transfers between devices with their start and end apart: 14, of which 3 were waited for; matrix products, arithmetic and copies ran while one was open for 9% of the time, Pallas kernels for 0%

profile of v1, /device:TPU:1, one launch (start us, length us, event | category | flops | bytes accessed | tf_op | source)
XLA Modules:
  0.0 553.6 jit_solution(16830958679058016174)
XLA Ops:
  6.5 1.7 reshape.78
  8.2 2.7 fusion.58
  10.9 3.1 copy.102
  14.0 4.7 collective-permute-start.4
  18.7 3.9 copy.105
  22.6 1.4 collective-permute-start.5
  24.0 1.1 fusion.59
  25.1 5.5 %collective-permute-start.2 = (f32[16,16,2,16]{3,2,1,0:T(2,128)}, f32[16,16,2,16]{3,2,1,0:T(2,128)}, u32[]{:S(2)}, u32[]{:S(2)}) collective-permute-start(f32[16,16,2,16]{3,2,1,0:T(2,128)} %get-tuple-element.31), channel_id=1, source_target_pairs={{0,32},{16,48},{32,64},{48,80},{64,96},{80,112},{96,128},{112,144}... | collective-permute-start | bytes 98312 | tf_op jit(solution)/shard_map/ppermute | solution.py:13
  30.6 1.4 collective-permute-start.3
  32.9 9.7 %collective-permute-start = (f32[16,2,16,16]{3,2,1,0:T(8,128)}, f32[16,2,16,16]{3,2,1,0:T(8,128)}, u32[]{:S(2)}, u32[]{:S(2)}) collective-permute-start(f32[16,2,16,16]{3,2,1,0:T(8,128)} %get-tuple-element.33), channel_id=1, source_target_pairs={{0,128},{16,144},{32,160},{48,176},{64,192},{80,208},{96,224},{112... | collective-permute-start | bytes 98312 | tf_op jit(solution)/shard_map/ppermute | solution.py:13
  42.6 2.0 copy.108
  44.6 4.4 gather_fusion
  50.5 1.0 copy.112
  51.5 1.3 collective-permute-start.1
  52.8 1.0 broadcast_multiply_fusion.8
  53.8 1.0 broadcast_multiply_fusion.3
  54.8 1.7 broadcast_multiply_fusion.1
  56.5 1.0 broadcast_multiply_fusion.12
  57.4 2.9 copy.104
  60.3 3.8 copy.107
  64.2 7.2 %collective-permute-done.1 = f32[16,2,16,16]{3,2,1,0:T(8,128)} collective-permute-done((f32[16,2,16,16]{3,2,1,0:T(8,128)}, f32[16,2,16,16]{3,2,1,0:T(8,128)}, u32[]{:S(2)}, u32[]{:S(2)}) %collective-permute-start.1) | collective-permute-done | bytes 32800 | tf_op jit(solution)/shard_map/ppermute | solution.py:13
  71.4 1.0 broadcast_multiply_fusion.10
  72.4 8.2 %fusion.20 = f32[16,16,16,16]{3,2,1,0:T(8,128)} fusion(f32[16,16,16,16]{3,2,1,0:T(8,128)S(1)} %reshape.78, f32[16,2,16,16]{3,2,1,0:T(8,128)S(1)} %broadcast_multiply_fusion.10, f32[16,2,16,16]{3,2,1,0:T(8,128)S(1)} %broadcast_multiply_fusion.12, f32[16,16,2,16]{3,2,1,0:T(2,128)S(1)} %bitcast.110, f32[16,16,2,16]{3,2,1,0:T(2,128)S(1)} %bitcast.108, ...), kind=kLoop, calls=%fused_computation.42 | loop fusion | flops 2097152 | bytes 720896 | tf_op jit(solution)/shard_map/mul | solution.py:62
  80.5 3.1 mul.170
  84.3 7.6 %scatter_fusion = f32[16,4096]{0,1:T(8,128)S(1)} fusion(f32[16,4096]{0,1:T(8,128)S(1)} %copy.111, s32[1024]{0:T(1024)S(1)} %bitcast.122, f32[1024,16]{1,0:T(8,128)} %copy.112), kind=kCustom, calls=%fused_computation.2 | custom fusion | flops 16384 | bytes 200704 | tf_op jit(solution)/shard_map/scatter-add | solution.py:44
  93.3 2.8 fusion.55
  96.1 1.1 fusion.56
  97.1 0.8 fusion.57
  98.0 2.0 copy.120
  99.9 3.1 copy.114
  103.1 2.0 collective-permute-start.10
  105.1 3.9 copy.117
  109.0 1.3 collective-permute-start.11
  110.2 4.1 collective-permute-start.8
  114.3 1.3 collective-permute-start.9
  115.6 13.3 %collective-permute-start.6 = (f32[16,2,16,16]{3,2,1,0:T(8,128)}, f32[16,2,16,16]{3,2,1,0:T(8,128)}, u32[]{:S(2)}, u32[]{:S(2)}) collective-permute-start(f32[16,2,16,16]{3,2,1,0:T(8,128)} %get-tuple-element.27), channel_id=1, source_target_pairs={{0,128},{16,144},{32,160},{48,176},{64,192},{80,208},{96,224},{112... | collective-permute-start | bytes 98312 | tf_op jit(solution)/shard_map/ppermute | solution.py:13
  128.9 4.4 gather_fusion.1
  134.1 1.0 copy.124
  135.1 1.3 collective-permute-start.7
  136.4 1.0 broadcast_multiply_fusion.7
  137.4 1.0 broadcast_multiply_fusion.5
  138.4 1.0 broadcast_multiply_fusion.2
  139.4 1.7 broadcast_multiply_fusion
  141.1 1.7 broadcast_multiply_fusion.11
  142.8 2.9 copy.116
  145.6 3.9 copy.119
  149.5 1.0 broadcast_multiply_fusion.9
  150.5 8.2 %fusion.9 = f32[16,16,16,16]{3,2,1,0:T(8,128)} fusion(f32[16,16,16,16]{3,2,1,0:T(8,128)S(1)} %reshape.81, f32[16,2,16,16]{3,2,1,0:T(8,128)S(1)} %broadcast_multiply_fusion.9, f32[16,2,16,16]{3,2,1,0:T(8,128)S(1)} %copy-done.2, f32[16,16,2,16]{3,2,1,0:T(2,128)S(1)} %bitcast.109, f32[16,16,2,16]{3,2,1,0:T(2,128)S(1)} %bitcast.107, ...), kind=kLoop, calls=%fused_computation.31 | loop fusion | flops 2097152 | bytes 720896 | tf_op jit(solution)/shard_map/mul | solution.py:62
  158.7 3.1 mul.188
  162.5 7.2 %scatter_fusion.1 = f32[16,4096]{0,1:T(8,128)S(1)} fusion(f32[16,4096]{0,1:T(8,128)S(1)} %copy.123, s32[1024]{0:T(1024)S(1)} %bitcast.123, f32[1024,16]{1,0:T(8,128)} %copy.124), kind=kCustom, calls=%fused_computation.3 | custom fusion | flops 16384 | bytes 200704 | tf_op jit(solution)/shard_map/scatter-add | solution.py:44
  170.4 20.5 %all_to_all.38 = f32[16,16,256]{2,0,1:T(8,128)S(1)} all-to-all(f32[16,16,256]{2,0,1:T(8,128)S(1)} %bitcast.112), channel_id=1, replica_groups=mesh['dom'=32,'band'=16] {'band'}, dimensions={1} | all-to-all | bytes 524288 | tf_op jit(solution)/shard_map/all_to_all | solution.py:66
  190.9 1.1 convolution_multiply_fusion
  192.1 111.0 %all-reduce.4.cloned.1.call-done = f32[256,256]{0,1:T(8,128)} async-done(((f32[256,256]{0,1:T(8,128)}), f32[256,256]{0,1:T(8,128)}) %all-reduce.4.cloned.1.call-update) | async-done | bytes 262160 | tf_op jit(solution)/shard_map/psum | solution.py:73
  303.2 157.0 %all-reduce.6.cloned.1.call-done = f32[256,256]{0,1:T(8,128)} async-done(((f32[256,256]{0,1:T(8,128)}), f32[256,256]{0,1:T(8,128)}) %all-reduce.6.cloned.1.call-update) | async-done | bytes 262160 | tf_op jit(solution)/shard_map/psum | solution.py:73
  460.2 1.1 copy.128
  461.3 1.0 fusion.44
  462.3 11.7 %cholesky.50 = f32[128,128]{1,0:T(8,128)S(1)} custom-call(f32[128,128]{1,0:T(8,128)S(1)} %cholesky.118), custom_call_target="Cholesky" | custom-call | tf_op jit(solution)/shard_map/jit(cholesky)/cholesky | solution.py:74
  474.0 9.8 %custom-call.15 = f32[1,128,128]{1,2,0:T(8,128)S(1)} custom-call(f32[1,128,128]{2,1,0:T(8,128)S(1)} %get-tuple-element.40), custom_call_target="InvertDiagBlocksLowerTriangular" | custom-call | tf_op jit(solution)/shard_map/jit(cholesky)/cholesky | solution.py:74
  484.3 11.7 %cholesky.105 = f32[128,128]{1,0:T(8,128)S(1)} custom-call(f32[128,128]{1,0:T(8,128)S(1)} %convolution_subtract_fusion.1), custom_call_target="Cholesky" | custom-call | tf_op jit(solution)/shard_map/jit(cholesky)/cholesky | solution.py:74
  498.0 4.0 while.1
  498.8 1.3 bitcast_dynamic-update-slice_fusion.2
  500.7 1.3 bitcast_dynamic-update-slice_fusion.2
  502.0 19.7 %custom-call.16 = f32[2,128,128]{1,2,0:T(8,128)S(1)} custom-call(f32[2,128,128]{2,1,0:T(8,128)S(1)} %get-tuple-element.12), custom_call_target="InvertDiagBlocksLowerTriangular" | custom-call | tf_op jit(solution)/shard_map/jit(_solve_triangular)/triangular_solve | solution.py:75
  522.7 23.1 %all_to_all.39 = f32[16,16,256]{2,1,0:T(8,128)S(1)} all-to-all(f32[16,16,256]{2,1,0:T(8,128)S(1)} %bitcast.111), channel_id=1, replica_groups=mesh['dom'=32,'band'=16] {'band'}, dimensions={0} | all-to-all | bytes 524288 | tf_op jit(solution)/shard_map/all_to_all | solution.py:76
  (84 shorter events, 10.6 us)
Async XLA Ops:
  6.5 43.2 %copy-start = (f32[4,8,256]{2,1,0:T(8,128)S(1)}, f32[4,8,256]{2,1,0:T(8,128)}, u32[]{:S(2)}) copy-start(f32[4,8,256]{2,1,0:T(8,128)} %param.8) | copy-start | bytes 98308
  6.5 296.6 %all-reduce.4.cloned.1.call-start = ((), (), s32[]{:S(2)}) async-start(), calls=%async_computation.2 | async-start | bytes 524288 | tf_op jit(solution)/shard_map/psum | solution.py:73
  14.0 39.8 %collective-permute-start.4 = (f32[16,16,16,2]{2,1,3,0:T(8,128)S(1)}, f32[16,16,16,2]{2,1,3,0:T(8,128)}, u32[]{:S(2)}, u32[]{:S(2)}) collective-permute-start(f32[16,16,16,2]{2,1,3,0:T(8,128)S(1)} %copy.102), channel_id=1, source_target_pairs={{0,16},{16,32},{32,48},{48,64},{64,80},{80,96},{96,112},{112,128},... | collective-permute-start | bytes 98312 | tf_op jit(solution)/shard_map/ppermute | solution.py:13
  18.7 23.9 %copy-start.1 = (f32[16,4096]{1,0:T(8,128)S(1)}, f32[16,4096]{1,0:T(8,128)}, u32[]{:S(2)}) copy-start(f32[16,4096]{1,0:T(8,128)} %param.5) | copy-start | bytes 786436
  22.6 21.9 %copy-start.9 = (s32[4,256]{1,0:T(4,128)S(1)}, s32[4,256]{1,0:T(4,128)}, u32[]{:S(2)}) copy-start(s32[4,256]{1,0:T(4,128)} %param.7) | copy-start | bytes 12292
  22.6 32.2 %collective-permute-start.5 = (f32[16,16,16,2]{2,1,3,0:T(8,128)}, f32[16,16,16,2]{2,1,3,0:T(8,128)}, u32[]{:S(2)}, u32[]{:S(2)}) collective-permute-start(f32[16,16,16,2]{2,1,3,0:T(8,128)} %copy.105), channel_id=1, source_target_pairs={{16,0},{32,16},{48,32},{64,48},{80,64},{96,80},{112,96},{128,112},... | collective-permute-start | bytes 98312 | tf_op jit(solution)/shard_map/ppermute | solution.py:13
  25.1 26.4 %collective-permute-start.2 = (f32[16,16,2,16]{3,2,1,0:T(2,128)}, f32[16,16,2,16]{3,2,1,0:T(2,128)}, u32[]{:S(2)}, u32[]{:S(2)}) collective-permute-start(f32[16,16,2,16]{3,2,1,0:T(2,128)} %get-tuple-element.31), channel_id=1, source_target_pairs={{0,32},{16,48},{32,64},{48,80},{64,96},{80,112},{96,128},{112,144}... | collective-permute-start | bytes 98312 | tf_op jit(solution)/shard_map/ppermute | solution.py:13
  30.6 19.1 %copy-start.4 = (f32[4096]{0:T(1024)S(1)}, f32[4096]{0:T(1024)}, u32[]{:S(2)}) copy-start(f32[4096]{0:T(1024)} %param.6) | copy-start | bytes 49156
  30.6 23.1 %collective-permute-start.3 = (f32[16,16,2,16]{3,2,1,0:T(2,128)}, f32[16,16,2,16]{3,2,1,0:T(2,128)S(1)}, u32[]{:S(2)}, u32[]{:S(2)}) collective-permute-start(f32[16,16,2,16]{3,2,1,0:T(2,128)} %get-tuple-element.32), channel_id=1, source_target_pairs={{32,0},{48,16},{64,32},{80,48},{96,64},{112,80},{128,96},{144,112}... | collective-permute-start | bytes 98312 | tf_op jit(solution)/shard_map/ppermute | solution.py:13
  32.9 17.1 %copy-start.3 = (f32[4,8,8]{2,1,0:T(8,128)S(1)}, f32[4,8,8]{2,1,0:T(8,128)}, u32[]{:S(2)}) copy-start(f32[4,8,8]{2,1,0:T(8,128)} %param.9) | copy-start | bytes 3076
  32.9 23.6 %collective-permute-start = (f32[16,2,16,16]{3,2,1,0:T(8,128)}, f32[16,2,16,16]{3,2,1,0:T(8,128)}, u32[]{:S(2)}, u32[]{:S(2)}) collective-permute-start(f32[16,2,16,16]{3,2,1,0:T(8,128)} %get-tuple-element.33), channel_id=1, source_target_pairs={{0,128},{16,144},{32,160},{48,176},{64,192},{80,208},{96,224},{112... | collective-permute-start | bytes 98312 | tf_op jit(solution)/shard_map/ppermute | solution.py:13
  44.6 4.6 copy-start.7
  51.5 19.9 %collective-permute-start.1 = (f32[16,2,16,16]{3,2,1,0:T(8,128)}, f32[16,2,16,16]{3,2,1,0:T(8,128)}, u32[]{:S(2)}, u32[]{:S(2)}) collective-permute-start(f32[16,2,16,16]{3,2,1,0:T(8,128)} %get-tuple-element.34), channel_id=1, source_target_pairs={{128,0},{144,16},{160,32},{176,48},{192,64},{208,80},{224,96},{240... | collective-permute-start | bytes 98312 | tf_op jit(solution)/shard_map/ppermute | solution.py:13
  83.7 0.7 copy-start.5
  99.9 29.0 %copy-start.8 = (s32[1024]{0:T(1024)S(1)}, s32[1024]{0:T(1024)}, u32[]{:S(2)}) copy-start(s32[1024]{0:T(1024)} %copy-done.7) | copy-start | bytes 12292
  103.1 35.3 %collective-permute-start.10 = (f32[16,16,16,2]{2,1,3,0:T(8,128)S(1)}, f32[16,16,16,2]{2,1,3,0:T(8,128)}, u32[]{:S(2)}, u32[]{:S(2)}) collective-permute-start(f32[16,16,16,2]{2,1,3,0:T(8,128)S(1)} %copy.114), channel_id=1, source_target_pairs={{0,16},{16,32},{32,48},{48,64},{64,80},{80,96},{96,112},{112,128},... | collective-permute-start | bytes 98312 | tf_op jit(solution)/shard_map/ppermute | solution.py:13
  109.0 30.4 %collective-permute-start.11 = (f32[16,16,16,2]{2,1,3,0:T(8,128)}, f32[16,16,16,2]{2,1,3,0:T(8,128)}, u32[]{:S(2)}, u32[]{:S(2)}) collective-permute-start(f32[16,16,16,2]{2,1,3,0:T(8,128)} %copy.117), channel_id=1, source_target_pairs={{16,0},{32,16},{48,32},{64,48},{80,64},{96,80},{112,96},{128,112},... | collective-permute-start | bytes 98312 | tf_op jit(solution)/shard_map/ppermute | solution.py:13
  110.2 24.9 %collective-permute-start.8 = (f32[16,16,2,16]{3,2,1,0:T(2,128)}, f32[16,16,2,16]{3,2,1,0:T(2,128)}, u32[]{:S(2)}, u32[]{:S(2)}) collective-permute-start(f32[16,16,2,16]{3,2,1,0:T(2,128)} %get-tuple-element.25), channel_id=1, source_target_pairs={{0,32},{16,48},{32,64},{48,80},{64,96},{80,112},{96,128},{112,144}... | collective-permute-start | bytes 98312 | tf_op jit(solution)/shard_map/ppermute | solution.py:13
  114.3 23.1 %collective-permute-start.9 = (f32[16,16,2,16]{3,2,1,0:T(2,128)}, f32[16,16,2,16]{3,2,1,0:T(2,128)}, u32[]{:S(2)}, u32[]{:S(2)}) collective-permute-start(f32[16,16,2,16]{3,2,1,0:T(2,128)} %get-tuple-element.26), channel_id=1, source_target_pairs={{32,0},{48,16},{64,32},{80,48},{96,64},{112,80},{128,96},{144,112}... | collective-permute-start | bytes 98312 | tf_op jit(solution)/shard_map/ppermute | solution.py:13
  115.6 25.5 %collective-permute-start.6 = (f32[16,2,16,16]{3,2,1,0:T(8,128)}, f32[16,2,16,16]{3,2,1,0:T(8,128)}, u32[]{:S(2)}, u32[]{:S(2)}) collective-permute-start(f32[16,2,16,16]{3,2,1,0:T(8,128)} %get-tuple-element.27), channel_id=1, source_target_pairs={{0,128},{16,144},{32,160},{48,176},{64,192},{80,208},{96,224},{112... | collective-permute-start | bytes 98312 | tf_op jit(solution)/shard_map/ppermute | solution.py:13
  135.1 14.4 %collective-permute-start.7 = (f32[16,2,16,16]{3,2,1,0:T(8,128)}, f32[16,2,16,16]{3,2,1,0:T(8,128)}, u32[]{:S(2)}, u32[]{:S(2)}) collective-permute-start(f32[16,2,16,16]{3,2,1,0:T(8,128)} %get-tuple-element.28), channel_id=1, source_target_pairs={{128,0},{144,16},{160,32},{176,48},{192,64},{208,80},{224,96},{240... | collective-permute-start | bytes 98312 | tf_op jit(solution)/shard_map/ppermute | solution.py:13
  145.6 4.9 copy-start.2
  161.8 0.7 copy-start.6
  192.0 268.1 %all-reduce.6.cloned.1.call-start = ((), (), s32[]{:S(2)}) async-start(), calls=%async_computation.3 | async-start | bytes 524288 | tf_op jit(solution)/shard_map/psum | solution.py:73
Sparse Core Ops, SparseCore 0:
  192.2 110.9 all-reduce.3
  306.6 153.5 all-reduce.5
